TPU v7x, 32 devices: a whole 2x2x4 slice. The times are simulated.
32 devices in a mesh: freq: 8 (over y, x, core), rcv: 4 (over z).
Axes of the slice: x: 2, y: 2, z: 4, core: 2. Of those that a mesh axis runs over, the one named last changes fastest.
Arguments:
- green_freq: float32 [2, 8, 2304, 2304], P(None, 'freq', 'rcv'), may hold values from -6 to 6
- data_matrix: float32 [2, 8, 2304, 2304], P(None, 'freq', 'rcv'), may hold values from -0.09375 to 0.09375
- shot_panels: float32 [2, 8, 2304, 256], P(None, 'freq', 'rcv'), may hold values from -6 to 6
- wavelet: float32 [2, 8], P(None, 'freq'), may hold values from -1.5 to 1.5
- sources: int32 [256], replicated, may hold values from 0 to 2303, as said below
- support: int32 [8, 2304], replicated, may hold values 0 or 1
- threshold: float32 [1], replicated, may hold values from 3 to 7
Outputs:
- green_next: float32 [2, 8, 2304, 2304], P(None, 'freq', 'rcv')
- residual: float32 [2, 8, 2304, 256], P(None, 'freq', 'rcv')
Inputs may be any that keep to these rules, and one draw needn't show every extreme that they name: `sources`: 256 distinct source positions. `support`: a 0/1 mask over time samples and source positions.
All inputs are finite; a program needn't handle non-finite values.
Results may differ from a plain program's by a relative error of at most 0.00013.
Values sent between devices are 32-bit elements; how exact they have to be, the bound alone decides.
A program may use at most 128 MiB of HBM per device.

v0:
```python
import math
import jax
import jax.numpy as jnp
from jax import lax
from jax.sharding import PartitionSpec as P

HIGHEST = lax.Precision.HIGHEST


def complex_product(left_pair, right_pair, pattern):
    left_real, left_imag = left_pair
    right_real, right_imag = right_pair
    real_part = jnp.einsum(pattern, left_real, right_real, precision=HIGHEST) - jnp.einsum(
        pattern, left_imag, right_imag, precision=HIGHEST
    )
    imag_part = jnp.einsum(pattern, left_real, right_imag, precision=HIGHEST) + jnp.einsum(
        pattern, left_imag, right_real, precision=HIGHEST
    )
    return (real_part, imag_part)


def conj_product(left_pair, right_pair, pattern):
    left_real, left_imag = left_pair
    right_real, right_imag = right_pair
    real_part = jnp.einsum(pattern, left_real, right_real, precision=HIGHEST) + jnp.einsum(
        pattern, left_imag, right_imag, precision=HIGHEST
    )
    imag_part = jnp.einsum(pattern, left_real, right_imag, precision=HIGHEST) - jnp.einsum(
        pattern, left_imag, right_real, precision=HIGHEST
    )
    return (real_part, imag_part)


def shrink_spectra(spectra, keep, shrink_level):
    n_freq = spectra.shape[1]
    grid = jnp.arange(n_freq, dtype=jnp.int32)
    phase = grid[:, None] * grid[None, :] % n_freq
    angle = phase.astype(jnp.float32) * (2.0 * math.pi / n_freq)
    cos_table = jnp.cos(angle)
    sin_table = jnp.sin(angle)
    pattern = "tf,f...->t..."
    time_real = jnp.einsum(pattern, cos_table, spectra[0], precision=HIGHEST) - jnp.einsum(
        pattern, sin_table, spectra[1], precision=HIGHEST
    )
    time_imag = jnp.einsum(pattern, sin_table, spectra[0], precision=HIGHEST) + jnp.einsum(
        pattern, cos_table, spectra[1], precision=HIGHEST
    )
    magnitude = jnp.sqrt(time_real * time_real + time_imag * time_imag)
    factor = (
        jnp.maximum(magnitude - shrink_level, 0.0) / jnp.maximum(magnitude, shrink_level) * keep
    )
    kept_real = factor * time_real
    kept_imag = factor * time_imag
    back_real = (
        jnp.einsum(pattern, cos_table, kept_real, precision=HIGHEST)
        + jnp.einsum(pattern, sin_table, kept_imag, precision=HIGHEST)
    ) / n_freq
    back_imag = (
        jnp.einsum(pattern, cos_table, kept_imag, precision=HIGHEST)
        - jnp.einsum(pattern, sin_table, kept_real, precision=HIGHEST)
    ) / n_freq
    return jnp.stack([back_real, back_imag])


def on_device(green_freq, data_matrix, shot_panels, wavelet, sources, support, threshold):
    data_pair = (data_matrix[0], data_matrix[1])
    picked = jnp.take(green_freq, sources, axis=3)
    wave_real = wavelet[0][:, None, None]
    wave_imag = wavelet[1][:, None, None]
    rows_here = green_freq.shape[2]
    shard_piece = lax.all_gather(picked, "rcv", axis=2, tiled=True)
    block_real = data_matrix[0]
    block_imag = data_matrix[1]
    real_part, imag_part = complex_product(
        (block_real, block_imag), (shard_piece[0], shard_piece[1]), "frk,fkc->frc"
    )
    multiple = jnp.stack([real_part, imag_part])
    resid_real = shot_panels[0] - (wave_real * picked[0] - wave_imag * picked[1] - multiple[0])
    resid_imag = shot_panels[1] - (wave_real * picked[1] + wave_imag * picked[0] - multiple[1])
    residual = jnp.stack([resid_real, resid_imag])
    local_real = wave_real * resid_real + wave_imag * resid_imag
    local_imag = wave_real * resid_imag - wave_imag * resid_real
    adj_real, adj_imag = conj_product(data_pair, (resid_real, resid_imag), "frk,frc->kfc")
    summed_terms = -jnp.stack([adj_real, adj_imag], axis=1)
    own_rows = jnp.transpose(jnp.stack([local_real, local_imag]), (2, 0, 1, 3))
    row_offset = lax.axis_index("rcv") * rows_here
    summed_terms = summed_terms + lax.dynamic_update_slice_in_dim(
        jnp.zeros_like(summed_terms), own_rows, row_offset, 0
    )
    summed_all = lax.psum(summed_terms, "rcv")
    mine = lax.dynamic_slice_in_dim(summed_all, row_offset, rows_here, 0)
    direction = jnp.transpose(mine, (1, 2, 0, 3))
    push_real, push_imag = complex_product(
        data_pair, (summed_all[:, 0], summed_all[:, 1]), "frk,kfc->frc"
    )
    pushed = jnp.stack([push_real, push_imag])
    image_real = wave_real * direction[0] - wave_imag * direction[1] - pushed[0]
    image_imag = wave_real * direction[1] + wave_imag * direction[0] - pushed[1]
    norm_dir = jnp.sum(direction * direction)
    norm_img = jnp.sum(image_real * image_real + image_imag * image_imag)
    totals = lax.psum((norm_dir, norm_img), ("freq", "rcv"))
    step_size = totals[0] / totals[1]
    updated = green_freq.at[:, :, :, sources].add(step_size * direction)
    keep_all = support.astype(jnp.float32)
    gathered = lax.all_to_all(updated, "freq", split_axis=2, concat_axis=1, tiled=True)
    shrunk = shrink_spectra(gathered, keep_all[:, None, :], threshold[0])
    green_next = lax.all_to_all(shrunk, "freq", split_axis=1, concat_axis=2, tiled=True)
    return (green_next, residual)


def solution(mesh):
    in_specs = (
        P(None, "freq", "rcv", None),
        P(None, "freq", "rcv", None),
        P(None, "freq", "rcv", None),
        P(None, "freq"),
        P(),
        P(),
        P(),
    )
    out_specs = (P(None, "freq", "rcv", None), P(None, "freq", "rcv", None))
    return jax.shard_map(
        on_device, mesh=mesh, in_specs=in_specs, out_specs=out_specs, check_vma=False
    )
```

profile of v0, /device:TPU:0, one launch (start us, length us, event | category | flops | bytes accessed | tf_op | source)
XLA Modules:
  0.0 851.4 jit_solution(611839117997585425)
XLA Ops:
  8.6 19.2 %copy.30 = f32[2,1,576,2304]{2,0,3,1:T(2,128)} copy(f32[2,1,576,2304]{3,2,1,0:T(8,128)} %param.7) | data formatting | bytes 21233664 | tf_op args[0]
  27.8 6.5 gather_fusion
  37.8 91.2 %all-gather.2.cloned.1.call-done = f32[2,1,2304,256]{3,2,1,0:T(8,128)} async-done(((f32[2,1,576,256]{3,2,1,0:T(8,128)}), f32[2,1,2304,256]{3,2,1,0:T(8,128)}) %all-gather.2.cloned.1.call-update) | async-done | bytes 4718608 | tf_op jit(solution)/shard_map/all_gather | solution.py:71
  129.0 7.5 fusion.8
  136.6 9.7 %fusion.101 = f32[576,256]{1,0:T(8,128)S(1)} fusion(f32[256,576]{0,1:T(8,128)S(1)} %fusion.8, f32[2,1,576,2304]{3,2,1,0:T(8,128)} %param.8, f32[2,1,2304,256]{3,2,1,0:T(8,128)} %all-gather.2.cloned.1.call-done, f32[2,1,576,256]{3,2,1,0:T(8,128)} %param.9, f32[2,1,576,256]{3,2,1,0:T(8,128)S(1)} %copy-done.2, f32[]{:T(128)} %bitcast.6, f32[]{:T(128)} %bitcast.3), kind=kOutput, calls=%fused_computation.76 | convolution fusion | flops 4077748224 | bytes 10617856 | tf_op jit(solution)/shard_map/frk,fkc->frc/dot_general | solution.py:16
  146.3 11.9 %fusion.6 = f32[256,2304]{0,1:T(8,128)S(1)} fusion(f32[576,256]{1,0:T(8,128)S(1)} %fusion.101, f32[2,1,576,2304]{3,2,1,0:T(8,128)} %param.8), kind=kOutput, calls=%fused_computation.9 | convolution fusion | flops 4076863488 | bytes 8257536 | tf_op jit(solution)/shard_map/frk,frc->kfc/dot_general | solution.py:25
  162.6 5.7 fusion.98
  168.3 9.6 %fusion.4 = f32[256,2304]{0,1:T(8,128)S(1)} fusion(f32[576,256]{1,0:T(8,128)S(1)} %fusion.98, f32[2,1,576,2304]{3,2,1,0:T(8,128)S(1)} %bitcast.238), kind=kOutput, calls=%fused_computation.7 | convolution fusion | flops 4076863488 | bytes 8257536 | tf_op jit(solution)/shard_map/frk,frc->kfc/dot_general | solution.py:28
  179.3 9.7 %fusion.41 = f32[2304,1,1,256]{3,0,2,1:T(8,128)S(1)} fusion(f32[256,2304]{0,1:T(8,128)S(1)} %fusion.6, f32[576,256]{1,0:T(8,128)S(1)} %fusion.98, f32[2,1,576,2304]{3,2,1,0:T(8,128)S(1)} %bitcast.238), kind=kOutput, calls=%fused_computation.44 | convolution fusion | flops 4077453312 | bytes 10616832 | tf_op jit(solution)/shard_map/frk,frc->kfc/dot_general | solution.py:25
  189.0 9.9 %fusion.38 = f32[2304,1,1,256]{3,0,2,1:T(8,128)S(1)} fusion(f32[256,2304]{0,1:T(8,128)S(1)} %fusion.4, f32[576,256]{1,0:T(8,128)S(1)} %fusion.101, f32[2,1,576,2304]{3,2,1,0:T(8,128)S(1)} %bitcast.238), kind=kOutput, calls=%fused_computation.43 | convolution fusion | flops 4077453312 | bytes 10616832 | tf_op jit(solution)/shard_map/frk,frc->kfc/dot_general | solution.py:28
  203.8 170.5 %all-reduce.3.cloned.1.call-done = f32[2304,2,1,256]{3,0,2,1:T(8,128)} async-done(((f32[2304,2,1,256]{3,0,2,1:T(8,128)}), f32[2304,2,1,256]{3,0,2,1:T(8,128)}) %all-reduce.3.cloned.1.call-update) | async-done | bytes 4718608 | tf_op jit(solution)/shard_map/psum | solution.py:90
  376.7 7.8 fusion
  384.5 7.0 fusion.2
  391.5 5.6 fusion.83
  397.2 6.3 fusion.109
  403.5 39.4 %all-reduce = (f32[]{:T(128)}, f32[]{:T(128)}) all-reduce(f32[]{:T(128)} %get-tuple-element.8, f32[]{:T(128)} %fusion.109), channel_id=1, replica_groups=mesh['freq'=8,'rcv'=4] {'freq','rcv'}, use_global_device_ids=true, to_apply=%region_2.3 | all-reduce | flops 2 | bytes 16 | tf_op jit(solution)/shard_map/psum | solution.py:101
  449.2 31.0 %scatter_fusion = f32[2,576,2304]{1,0,2:T(2,128)} fusion(f32[2,576,2304]{1,0,2:T(2,128)} %bitcast.242, s32[256]{0:T(256)S(1)} %compare_select_fusion, f32[256,2,576]{2,1,0:T(2,128)S(1)} %copy.36), kind=kCustom, calls=%fused_computation.1 | custom fusion | flops 294912 | bytes 3539968 | tf_op jit(solution)/shard_map/scatter-add | solution.py:103
  480.3 21.2 %copy.37 = f32[2,1,576,2304]{3,0,1,2:T(2,128)} copy(f32[2,1,576,2304]{2,0,3,1:T(2,128)} %bitcast.243) | data formatting | bytes 21233664 | tf_op jit(solution)/shard_map/scatter-add | solution.py:103
  501.5 5.3 all-to-all-start
  507.5 117.2 %all-to-all-done = f32[2,1,576,2304]{3,0,1,2:T(2,128)} async-done(((f32[2,1,576,2304]{3,0,1,2:T(2,128)}), f32[2,1,576,2304]{3,0,1,2:T(2,128)}, u32[]{:S(2)}, u32[]{:S(2)}) %all-to-all-start) | async-done | bytes 10616864 | tf_op jit(solution)/shard_map/all_to_all | solution.py:105
  624.7 12.6 %fusion.174 = (f32[1,1,576,2304]{3,0,1,2:T(1,128)S(1)}, f32[1,1,576,2304]{3,0,1,2:T(1,128)S(1)}) fusion(f32[2,1,576,2304]{3,0,1,2:T(2,128)} %all-to-all-done), kind=kLoop, calls=%fused_computation.145 | loop fusion | bytes 21233664 | tf_op jit(solution)/shard_map/slice | solution.py:43
  637.7 7.0 fusion.30
  644.7 7.0 fusion.28
  652.1 7.1 convolution_subtract_fusion
  659.2 7.4 convolution_add_fusion
  666.6 7.6 fusion.121
  674.3 8.0 fusion.119
  682.3 8.8 %multiply_bitcast_fusion.1 = f32[1,8,72,2304]{3,1,2,0:T(8,128)} fusion(f32[8,72,2304]{2,0,1:T(8,128)S(1)} %fusion.121, f32[8,72,2304]{2,0,1:T(8,128)S(1)} %convolution_add_fusion, f32[8,72,2304]{2,0,1:T(8,128)S(1)} %convolution_subtract_fusion, f32[8,2304]{1,0:T(8,128)S(1)} %convert_element_type.21, f32[]{:T(128)} %bitcast.234), kind=kOutput, calls=%fused_computation.28 | convolution fusion | flops 142001024 | bytes 21307396 | tf_op jit(solution)/shard_map/tf,f...->t.../dot_general | solution.py:56
  691.1 9.0 %multiply_bitcast_fusion = f32[1,8,72,2304]{3,1,2,0:T(8,128)} fusion(f32[8,72,2304]{2,0,1:T(8,128)S(1)} %fusion.119, f32[8,72,2304]{2,0,1:T(8,128)S(1)} %convolution_subtract_fusion, f32[8,72,2304]{2,0,1:T(8,128)S(1)} %convolution_add_fusion, f32[8,2304]{1,0:T(8,128)S(1)} %convert_element_type.21, f32[]{:T(128)} %bitcast.235), kind=kOutput, calls=%fused_computation.27 | convolution fusion | flops 142001024 | bytes 21307396 | tf_op jit(solution)/shard_map/tf,f...->t.../dot_general | solution.py:60
  704.9 7.4 copy.44
  718.5 116.8 %all-to-all-done.1 = f32[2,8,72,2304]{3,2,0,1:T(8,128)} async-done(((f32[2,8,72,2304]{3,2,0,1:T(8,128)}), f32[2,8,72,2304]{3,2,0,1:T(8,128)}, u32[]{:S(2)}, u32[]{:S(2)}) %all-to-all-start.1) | async-done | bytes 10616864 | tf_op jit(solution)/shard_map/all_to_all | solution.py:107
  835.3 9.0 %copy.45 = f32[2,8,72,2304]{3,2,1,0:T(8,128)} copy(f32[2,8,72,2304]{3,2,0,1:T(8,128)} %all-to-all-done.1) | data formatting | bytes 21233664 | tf_op jit(solution)/shard_map/all_to_all | solution.py:107
  (54 shorter events, 34.6 us)
Async XLA Ops:
  7.2 121.9 %all-gather.2.cloned.1.call-start = ((), (), s32[]{:S(2)}) async-start(), calls=%async_computation.2 | async-start | bytes 5898240 | tf_op jit(solution)/shard_map/all_gather | solution.py:71
  27.8 9.3 %copy-start.5 = (f32[2,1]{0,1:T(1,128)S(1)}, f32[2,1]{0,1:T(1,128)}, u32[]{:S(2)}) copy-start(f32[2,1]{0,1:T(1,128)} %param.10) | copy-start | bytes 28
  36.7 99.8 %copy-start.2 = (f32[2,1,576,256]{3,2,1,0:T(8,128)S(1)}, f32[2,1,576,256]{3,2,1,0:T(8,128)}, u32[]{:S(2)}) copy-start(f32[2,1,576,256]{3,2,1,0:T(8,128)} %bitcast_select_fusion) | copy-start | bytes 3538948
  36.8 337.6 %all-reduce.3.cloned.1.call-start = ((), (), s32[]{:S(2)}) async-start(), calls=%async_computation.3 | async-start | bytes 9437184 | tf_op jit(solution)/shard_map/psum | solution.py:90
  129.0 29.2 %slice-start = ((s8[10616832]{0:T(1024)(128)(4,1)}), s8[4194304]{0:T(1024)(128)(4,1)S(1)}, s32[]{:S(2)}) async-start(s8[10616832]{0:T(1024)(128)(4,1)} %bitcast.237), calls=%async_computation.4 | async-start | bytes 8388608
  129.0 29.2 %slice-start.6 = ((s8[4718592]{0:T(1024)(128)(4,1)}), s8[4194304]{0:T(1024)(128)(4,1)S(1)}, s32[]{:S(2)}) async-start(s8[4718592]{0:T(1024)(128)(4,1)} %bitcast.248), calls=%async_computation.10 | async-start | bytes 8388608
  136.5 21.7 %slice-start.1 = ((s8[10616832]{0:T(1024)(128)(4,1)}), s8[4194304]{0:T(1024)(128)(4,1)S(1)}, s32[]{:S(2)}) async-start(s8[10616832]{0:T(1024)(128)(4,1)} %bitcast.237), calls=%async_computation.5 | async-start | bytes 8388608
  136.5 21.7 %slice-start.2 = ((s8[10616832]{0:T(1024)(128)(4,1)}), s8[2228224]{0:T(1024)(128)(4,1)S(1)}, s32[]{:S(2)}) async-start(s8[10616832]{0:T(1024)(128)(4,1)} %bitcast.237), calls=%async_computation.6 | async-start | bytes 4456448
  136.5 21.7 %slice-start.7 = ((s8[4718592]{0:T(1024)(128)(4,1)}), s8[524288]{0:T(1024)(128)(4,1)S(1)}, s32[]{:S(2)}) async-start(s8[4718592]{0:T(1024)(128)(4,1)} %bitcast.248), calls=%async_computation.11 | async-start | bytes 1048576
  158.2 4.4 copy-start.3
  203.8 187.7 %slice-start.3 = ((s8[10616832]{0:T(1024)(128)(4,1)}), s8[2228224]{0:T(1024)(128)(4,1)S(1)}, s32[]{:S(2)}) async-start(s8[10616832]{0:T(1024)(128)(4,1)} %bitcast.239), calls=%async_computation.7 | async-start | bytes 4456448
  374.4 10.2 %copy-start = (f32[2304,2,1,256]{3,0,2,1:T(8,128)S(1)}, f32[2304,2,1,256]{3,0,2,1:T(8,128)}, u32[]{:S(2)}) copy-start(f32[2304,2,1,256]{3,0,2,1:T(8,128)} %all-reduce.3.cloned.1.call-done) | copy-start | bytes 14155780
  376.7 20.5 %copy-start.1 = (f32[2,1,576,256]{3,2,1,0:T(8,128)}, f32[2,1,576,256]{3,2,1,0:T(8,128)S(1)}, u32[]{:S(2)}) copy-start(f32[2,1,576,256]{3,2,1,0:T(8,128)S(1)} %get-tuple-element.9) | copy-start | bytes 3538948
  376.7 14.8 %slice-start.4 = ((s8[10616832]{0:T(1024)(128)(4,1)}), s8[4194304]{0:T(1024)(128)(4,1)S(1)}, s32[]{:S(2)}) async-start(s8[10616832]{0:T(1024)(128)(4,1)} %bitcast.239), calls=%async_computation.8 | async-start | bytes 8388608
  384.5 7.0 slice-start.5
  501.5 5.3 copy-start.4
  501.5 123.2 %all-to-all-start = ((f32[2,1,576,2304]{3,0,1,2:T(2,128)}), f32[2,1,576,2304]{3,0,1,2:T(2,128)}, u32[]{:S(2)}, u32[]{:S(2)}) async-start(f32[2,1,576,2304]{3,0,1,2:T(2,128)} %copy.37), calls=%async_computation | async-start | bytes 21233664 | tf_op jit(solution)/shard_map/all_to_all | solution.py:105
  712.2 123.1 %all-to-all-start.1 = ((f32[2,8,72,2304]{3,2,0,1:T(8,128)}), f32[2,8,72,2304]{3,2,0,1:T(8,128)}, u32[]{:S(2)}, u32[]{:S(2)}) async-start(f32[2,8,72,2304]{3,2,0,1:T(8,128)} %copy.44), calls=%async_computation.1 | async-start | bytes 21233664 | tf_op jit(solution)/shard_map/all_to_all | solution.py:107
Sparse Core Ops, SparseCore 0:
  36.9 92.0 all-gather.1
  203.9 170.3 all-reduce.2
where the time goes:
time: 856 us; the launch traced here: 851 us
  waiting for transfers between devices  496 us (58%)
  matrix products  157 us (18%)
  local copies, waits for them, and re-layouts  81.3 us (9%)
  other arithmetic  50.4 us (6%)
  blocking collectives  39.4 us (5%)
  between operations  16.6 us (2%)
  starting transfers between devices  10.8 us (1%)
    psum x1, waiting for transfers between devices, on_device(): summed_all = lax.psum(summed_terms, 'rcv')  171 us
    all_to_all x1, waiting for transfers between devices, on_device(): lax.all_to_all(updated, 'freq', split_axis=2, concat_axis=1, tiled=True)  117 us
    all_to_all x1, waiting for transfers between devices, on_device(): lax.all_to_all(shrunk, 'freq', split_axis=1, concat_axis=2, tiled=True)  117 us
    all_gather x1, waiting for transfers between devices, on_device(): shard_piece = lax.all_gather(picked, 'rcv', axis=2, tiled=True)  91.2 us
    psum x1, blocking collectives, on_device(): totals = lax.psum((norm_dir, norm_img), ('freq', 'rcv'))  39.4 us
    scatter-add x1, other arithmetic, on_device(): updated = green_freq.at[:, :, :, sources].add(step_size * direction)  31 us
    scatter-add x1, local copies, waits for them, and re-layouts, on_device(): updated = green_freq.at[:, :, :, sources].add(step_size * direction)  21.2 us
    unnamed x31, local copies, waits for them, and re-layouts  20 us
  transfers between devices with their start and end apart: 4, of which 4 were waited for; matrix products, arithmetic and copies ran while one was open for 0% of the time, Pallas kernels for 0%

commit v1 on v0

--- a/solution.py
+++ b/solution.py
@@ -5,6 +5,15 @@
 from jax.sharding import PartitionSpec as P
 
 HIGHEST = lax.Precision.HIGHEST
+
+
+def added_up(block, axis):
+    count = lax.axis_size(axis)
+    acc, far = (block, 1)
+    while far < count:
+        acc = acc + lax.ppermute(acc, axis, [(i, i ^ far) for i in range(count)])
+        far = 2 * far
+    return acc
 
 
 def complex_product(left_pair, right_pair, pattern):
@@ -87,7 +96,7 @@
     summed_terms = summed_terms + lax.dynamic_update_slice_in_dim(
         jnp.zeros_like(summed_terms), own_rows, row_offset, 0
     )
-    summed_all = lax.psum(summed_terms, "rcv")
+    summed_all = added_up(summed_terms, "rcv")
     mine = lax.dynamic_slice_in_dim(summed_all, row_offset, rows_here, 0)
     direction = jnp.transpose(mine, (1, 2, 0, 3))
     push_real, push_imag = complex_product(

time: 856 us -> 986 us (1.15)
  waiting for transfers between devices: 496 us -> 633 us
    ppermute x0 -> x2, waiting for transfers between devices: none -> 307 us  [added_up(): acc = acc + lax.ppermute(acc, axis, [(i, i ^ far) for i in range(count)])]
    psum x1 -> x0, waiting for transfers between devices: 171 us -> none  [on_device(): summed_all = lax.psum(summed_terms, 'rcv')]
    unnamed x31 -> x21, local copies, waits for them, and re-layouts: 20 us -> 20 us
  transfers between devices with their start and end apart: 4 -> 5, of which waited for: 4 -> 5; matrix products, arithmetic and copies ran while one was open for 0% -> 0% of each run, Pallas kernels for 0% -> 0%
where the time goes in v1:
time: 986 us; the launch traced here: 978 us
  waiting for transfers between devices  633 us (64%)
  matrix products  153 us (16%)
  local copies, waits for them, and re-layouts  81.1 us (8%)
  other arithmetic  44.6 us (5%)
  blocking collectives  38 us (4%)
  between operations  16.6 us (2%)
  starting transfers between devices  11.4 us (1%)
    ppermute x2, waiting for transfers between devices, added_up(): acc = acc + lax.ppermute(acc, axis, [(i, i ^ far) for i in range(count)])  307 us
    all_to_all x1, waiting for transfers between devices, on_device(): lax.all_to_all(updated, 'freq', split_axis=2, concat_axis=1, tiled=True)  117 us
    all_to_all x1, waiting for transfers between devices, on_device(): lax.all_to_all(shrunk, 'freq', split_axis=1, concat_axis=2, tiled=True)  117 us
    all_gather x1, waiting for transfers between devices, on_device(): shard_piece = lax.all_gather(picked, 'rcv', axis=2, tiled=True)  91.6 us
    psum x1, blocking collectives, on_device(): totals = lax.psum((norm_dir, norm_img), ('freq', 'rcv'))  38 us
    scatter-add x1, other arithmetic, on_device(): updated = green_freq.at[:, :, :, sources].add(step_size * direction)  31 us
    scatter-add x1, local copies, waits for them, and re-layouts, on_device(): updated = green_freq.at[:, :, :, sources].add(step_size * direction)  21.2 us
    unnamed x21, local copies, waits for them, and re-layouts  20 us
  transfers between devices with their start and end apart: 5, of which 5 were waited for; matrix products, arithmetic and copies ran while one was open for 0% of the time, Pallas kernels for 0%

profile of v1, /device:TPU:0, one launch (start us, length us, event | category | flops | bytes accessed | tf_op | source)
XLA Modules:
  0.0 978.2 jit_solution(17173900649147646454)
XLA Ops:
  8.6 19.2 %copy.30 = f32[2,1,576,2304]{2,0,3,1:T(2,128)} copy(f32[2,1,576,2304]{3,2,1,0:T(8,128)} %param.7) | data formatting | bytes 21233664 | tf_op args[0]
  27.8 6.5 gather_fusion
  37.4 91.6 %all-gather.2.cloned.1.call-done = f32[2,1,2304,256]{3,2,1,0:T(8,128)} async-done(((f32[2,1,576,256]{3,2,1,0:T(8,128)}), f32[2,1,2304,256]{3,2,1,0:T(8,128)}) %all-gather.2.cloned.1.call-update) | async-done | bytes 4718608 | tf_op jit(solution)/shard_map/all_gather | solution.py:80
  129.0 7.5 fusion.8
  136.6 9.4 fusion.101
  146.0 11.8 %fusion.6 = f32[256,2304]{0,1:T(8,128)S(1)} fusion(f32[576,256]{1,0:T(8,128)S(1)} %fusion.101, f32[2,1,576,2304]{3,2,1,0:T(8,128)} %param.8), kind=kOutput, calls=%fused_computation.9 | convolution fusion | flops 4076863488 | bytes 8257536 | tf_op jit(solution)/shard_map/frk,frc->kfc/dot_general | solution.py:34
  162.3 5.8 fusion.98
  168.1 10.4 %fusion.4 = f32[256,2304]{0,1:T(8,128)S(1)} fusion(f32[576,256]{1,0:T(8,128)S(1)} %fusion.98, f32[2,1,576,2304]{3,2,1,0:T(8,128)S(1)} %bitcast.238), kind=kOutput, calls=%fused_computation.7 | convolution fusion | flops 4076863488 | bytes 8257536 | tf_op jit(solution)/shard_map/frk,frc->kfc/dot_general | solution.py:37
  179.9 10.5 %fusion.41 = f32[2304,1,1,256]{3,0,2,1:T(8,128)S(1)} fusion(f32[256,2304]{0,1:T(8,128)S(1)} %fusion.6, f32[576,256]{1,0:T(8,128)S(1)} %fusion.98, f32[2,1,576,2304]{3,2,1,0:T(8,128)S(1)} %bitcast.238), kind=kOutput, calls=%fused_computation.44 | convolution fusion | flops 4077453312 | bytes 10616832 | tf_op jit(solution)/shard_map/frk,frc->kfc/dot_general | solution.py:34
  190.4 10.7 %fusion.38 = f32[2304,1,1,256]{3,0,2,1:T(8,128)S(1)} fusion(f32[256,2304]{0,1:T(8,128)S(1)} %fusion.4, f32[576,256]{1,0:T(8,128)S(1)} %fusion.101, f32[2,1,576,2304]{3,2,1,0:T(8,128)S(1)} %bitcast.238), kind=kOutput, calls=%fused_computation.43 | convolution fusion | flops 4077453312 | bytes 10616832 | tf_op jit(solution)/shard_map/frk,frc->kfc/dot_general | solution.py:37
  201.7 103.5 %collective-permute-done = f32[2304,2,1,256]{3,0,2,1:T(8,128)S(1)} collective-permute-done((f32[2304,2,1,256]{3,0,2,1:T(8,128)S(1)}, f32[2304,2,1,256]{3,0,2,1:T(8,128)S(1)}, u32[]{:S(2)}, u32[]{:S(2)}) %collective-permute-start) | collective-permute-done | bytes 4718624 | tf_op jit(solution)/shard_map/ppermute | solution.py:14
  306.6 203.9 %collective-permute-done.1 = f32[2304,2,1,256]{3,0,2,1:T(8,128)S(1)} collective-permute-done((f32[2304,2,1,256]{3,0,2,1:T(8,128)S(1)}, f32[2304,2,1,256]{3,0,2,1:T(8,128)S(1)}, u32[]{:S(2)}, u32[]{:S(2)}) %collective-permute-start.1) | collective-permute-done | bytes 4718624 | tf_op jit(solution)/shard_map/ppermute | solution.py:14
  521.0 5.7 fusion.83
  526.7 6.4 fusion.109
  533.1 38.0 %all-reduce = (f32[]{:T(128)}, f32[]{:T(128)}) all-reduce(f32[]{:T(128)} %get-tuple-element.8, f32[]{:T(128)} %fusion.109), channel_id=1, replica_groups=mesh['freq'=8,'rcv'=4] {'freq','rcv'}, use_global_device_ids=true, to_apply=%region_1.2 | all-reduce | flops 2 | bytes 16 | tf_op jit(solution)/shard_map/psum | solution.py:110
  576.2 31.0 %scatter_fusion = f32[2,576,2304]{1,0,2:T(2,128)} fusion(f32[2,576,2304]{1,0,2:T(2,128)} %bitcast.240, s32[256]{0:T(256)S(1)} %compare_select_fusion, f32[256,2,576]{2,1,0:T(2,128)S(1)} %copy.36), kind=kCustom, calls=%fused_computation.1 | custom fusion | flops 294912 | bytes 3539968 | tf_op jit(solution)/shard_map/scatter-add | solution.py:112
  607.2 21.2 %copy.37 = f32[2,1,576,2304]{3,0,1,2:T(2,128)} copy(f32[2,1,576,2304]{2,0,3,1:T(2,128)} %bitcast.241) | data formatting | bytes 21233664 | tf_op jit(solution)/shard_map/scatter-add | solution.py:112
  628.5 5.3 all-to-all-start
  634.4 117.2 %all-to-all-done = f32[2,1,576,2304]{3,0,1,2:T(2,128)} async-done(((f32[2,1,576,2304]{3,0,1,2:T(2,128)}), f32[2,1,576,2304]{3,0,1,2:T(2,128)}, u32[]{:S(2)}, u32[]{:S(2)}) %all-to-all-start) | async-done | bytes 10616864 | tf_op jit(solution)/shard_map/all_to_all | solution.py:114
  751.7 12.4 %fusion.174 = (f32[1,1,576,2304]{3,0,1,2:T(1,128)S(1)}, f32[1,1,576,2304]{3,0,1,2:T(1,128)S(1)}) fusion(f32[2,1,576,2304]{3,0,1,2:T(2,128)} %all-to-all-done), kind=kLoop, calls=%fused_computation.145 | loop fusion | bytes 21233664 | tf_op jit(solution)/shard_map/slice | solution.py:52
  764.5 7.0 fusion.30
  771.5 7.0 fusion.28
  778.9 7.1 convolution_subtract_fusion
  786.0 7.4 convolution_add_fusion
  793.4 7.6 fusion.121
  801.1 8.0 fusion.119
  809.1 8.8 multiply_bitcast_fusion.1
  817.9 9.0 multiply_bitcast_fusion
  831.7 7.4 copy.44
  839.0 5.2 all-to-all-start.1
  845.3 116.8 %all-to-all-done.1 = f32[2,8,72,2304]{3,2,0,1:T(8,128)} async-done(((f32[2,8,72,2304]{3,2,0,1:T(8,128)}), f32[2,8,72,2304]{3,2,0,1:T(8,128)}, u32[]{:S(2)}, u32[]{:S(2)}) %all-to-all-start.1) | async-done | bytes 10616864 | tf_op jit(solution)/shard_map/all_to_all | solution.py:116
  962.1 9.0 copy.45
  (46 shorter events, 33.1 us)
Async XLA Ops:
  7.2 121.9 %all-gather.2.cloned.1.call-start = ((), (), s32[]{:S(2)}) async-start(), calls=%async_computation.2 | async-start | bytes 5898240 | tf_op jit(solution)/shard_map/all_gather | solution.py:80
  27.8 8.9 copy-start.3
  36.7 99.8 %copy-start = (f32[2,1,576,256]{3,2,1,0:T(8,128)S(1)}, f32[2,1,576,256]{3,2,1,0:T(8,128)}, u32[]{:S(2)}) copy-start(f32[2,1,576,256]{3,2,1,0:T(8,128)} %bitcast_select_fusion) | copy-start | bytes 3538948
  36.7 99.8 %copy-start.1 = (f32[2,1,576,256]{3,2,1,0:T(8,128)S(1)}, f32[2,1,576,256]{3,2,1,0:T(8,128)}, u32[]{:S(2)}) copy-start(f32[2,1,576,256]{3,2,1,0:T(8,128)} %param.9) | copy-start | bytes 3538948
  129.0 28.8 %slice-start = ((s8[10616832]{0:T(1024)(128)(4,1)}), s8[4194304]{0:T(1024)(128)(4,1)S(1)}, s32[]{:S(2)}) async-start(s8[10616832]{0:T(1024)(128)(4,1)} %bitcast.237), calls=%async_computation.3 | async-start | bytes 8388608
  129.0 28.8 %slice-start.3 = ((s8[4718592]{0:T(1024)(128)(4,1)}), s8[4194304]{0:T(1024)(128)(4,1)S(1)}, s32[]{:S(2)}) async-start(s8[4718592]{0:T(1024)(128)(4,1)} %bitcast.246), calls=%async_computation.6 | async-start | bytes 8388608
  136.5 21.3 %slice-start.1 = ((s8[10616832]{0:T(1024)(128)(4,1)}), s8[4194304]{0:T(1024)(128)(4,1)S(1)}, s32[]{:S(2)}) async-start(s8[10616832]{0:T(1024)(128)(4,1)} %bitcast.237), calls=%async_computation.4 | async-start | bytes 8388608
  136.5 21.3 %slice-start.2 = ((s8[10616832]{0:T(1024)(128)(4,1)}), s8[2228224]{0:T(1024)(128)(4,1)S(1)}, s32[]{:S(2)}) async-start(s8[10616832]{0:T(1024)(128)(4,1)} %bitcast.237), calls=%async_computation.5 | async-start | bytes 4456448
  136.6 21.3 %slice-start.4 = ((s8[4718592]{0:T(1024)(128)(4,1)}), s8[524288]{0:T(1024)(128)(4,1)S(1)}, s32[]{:S(2)}) async-start(s8[4718592]{0:T(1024)(128)(4,1)} %bitcast.246), calls=%async_computation.7 | async-start | bytes 1048576
  201.6 103.6 %collective-permute-start = (f32[2304,2,1,256]{3,0,2,1:T(8,128)S(1)}, f32[2304,2,1,256]{3,0,2,1:T(8,128)S(1)}, u32[]{:S(2)}, u32[]{:S(2)}) collective-permute-start(f32[2304,2,1,256]{3,0,2,1:T(8,128)S(1)} %fusion.108), channel_id=1, source_target_pairs={{0,1},{1,0},{2,3},{3,2},{4,5},{5,4},{6,7},{7,6},{8,9},{9,8},{10,11... | collective-permute-start | bytes 14155784 | tf_op jit(solution)/shard_map/ppermute | solution.py:14
  305.8 204.7 %collective-permute-start.1 = (f32[2304,2,1,256]{3,0,2,1:T(8,128)S(1)}, f32[2304,2,1,256]{3,0,2,1:T(8,128)S(1)}, u32[]{:S(2)}, u32[]{:S(2)}) collective-permute-start(f32[2304,2,1,256]{3,0,2,1:T(8,128)S(1)} %add.117), channel_id=1, source_target_pairs={{0,2},{1,3},{2,0},{3,1},{4,6},{5,7},{6,4},{7,5},{8,10},{9,11},{10,... | collective-permute-start | bytes 14155784 | tf_op jit(solution)/shard_map/ppermute | solution.py:14
  628.4 5.3 copy-start.2
  628.5 123.2 %all-to-all-start = ((f32[2,1,576,2304]{3,0,1,2:T(2,128)}), f32[2,1,576,2304]{3,0,1,2:T(2,128)}, u32[]{:S(2)}, u32[]{:S(2)}) async-start(f32[2,1,576,2304]{3,0,1,2:T(2,128)} %copy.37), calls=%async_computation | async-start | bytes 21233664 | tf_op jit(solution)/shard_map/all_to_all | solution.py:114
  839.0 123.1 %all-to-all-start.1 = ((f32[2,8,72,2304]{3,2,0,1:T(8,128)}), f32[2,8,72,2304]{3,2,0,1:T(8,128)}, u32[]{:S(2)}, u32[]{:S(2)}) async-start(f32[2,8,72,2304]{3,2,0,1:T(8,128)} %copy.44), calls=%async_computation.1 | async-start | bytes 21233664 | tf_op jit(solution)/shard_map/all_to_all | solution.py:116
Sparse Core Ops, SparseCore 0:
  36.9 92.0 all-gather.1
